TPU v7x, 128 devices: a whole 4x4x4 slice. The times are simulated.
128 devices in a mesh: grp: 4 (over x), seq: 32 (over y, z, core).
Axes of the slice: x: 4, y: 4, z: 4, core: 2. Of those that a mesh axis runs over, the one named last changes fastest.
Arguments:
- grad_output: bfloat16 [4096, 8192], P('seq', 'grp'), may hold values from -6 to 6
- hidden: bfloat16 [4096, 28672], P('seq', 'grp'), may hold values from -6 to 6
- down_weight: bfloat16 [28672, 8192], P('seq', 'grp'), may hold values from -0.0625 to 0.0625
- adapter_down: bfloat16 [64, 64, 28672], P(None, None, ('grp', 'seq')), may hold values from -0.03125 to 0.03125
- adapter_up: bfloat16 [64, 64, 8192], P(None, None, ('grp', 'seq')), may hold values from -0.0625 to 0.0625
- job_tenant: int32 [32, 4], replicated, may hold values from 0 to 63, all different within a row
- job_count: int32 [32, 4], replicated, may hold values from 1 to 64, 128 in all within a row
Outputs:
- grad_hidden: bfloat16 [4096, 28672], P('seq', 'grp')
- grad_adapter_down: float32 [64, 64, 28672], P(None, None, ('grp', 'seq'))
- grad_adapter_up: float32 [64, 64, 8192], P(None, None, ('grp', 'seq'))
Inputs may be any that keep to these rules, and one draw needn't show every extreme that they name: `job_tenant`: each row names 4 different tenants; every tenant is named by some row. `job_count`: each row sums to 128, and its largest entry is exactly 64.
All inputs are finite; a program needn't handle non-finite values.
Results may differ from a plain program's by a relative error of at most 0.015.
Values may be sent and summed in bfloat16 or wider, within the bound.
A program may use at most 128 MiB of HBM per device.

v0:
```python
import jax
import jax.numpy as jnp
from jax import lax
from jax.sharding import PartitionSpec as P

ADAPTER_SCALE = 2.0


def shards(grad_output, hidden, down_weight, adapter_down, adapter_up, job_tenant, job_count):
    shard_index = lax.axis_index(SEQ)
    shard_count = lax.axis_size(SEQ)
    group_count = lax.axis_size("grp")
    tok_rows = grad_output.shape[0]
    job_slots = job_tenant.shape[1]
    ranks = adapter_down.shape[1]
    down_slab = adapter_down.shape[2]
    up_slab = adapter_up.shape[2]
    tenant_total = adapter_down.shape[0]
    contract_last = (((1,), (1,)), ((), ()))
    contract_rows = (((0,), (0,)), ((), ()))
    tenant_table = (
        job_tenant[:, :, None] == lax.broadcasted_iota(jnp.int32, (1, 1, tenant_total), 2)
    ).astype(jnp.float32)
    totals = jnp.sum(job_count.astype(jnp.float32)[:, :, None] * tenant_table, axis=(0, 1))
    weights = ADAPTER_SCALE / totals
    table_here = lax.dynamic_index_in_dim(tenant_table, shard_index, 0, keepdims=False)
    job_weights = jnp.sum(table_here * weights[None, :], axis=1)
    counts_here = lax.dynamic_index_in_dim(job_count, shard_index, 0, keepdims=False)
    run_ends = jnp.cumsum(counts_here)
    run_starts = run_ends - counts_here
    positions = lax.broadcasted_iota(jnp.int32, (tok_rows, job_slots), 0)
    member = ((positions >= run_starts[None, :]) & (positions < run_ends[None, :])).astype(
        jnp.float32
    )
    chosen = job_tenant.T
    fetched_down, fetched_up = (
        lax.all_to_all(adapter_down[chosen], SEQ, split_axis=1, concat_axis=3, tiled=True),
        lax.all_to_all(adapter_up[chosen], SEQ, split_axis=1, concat_axis=3, tiled=True),
    )
    down_stack = fetched_down.reshape(job_slots * ranks, shard_count * down_slab)
    up_stack = fetched_up.reshape(job_slots * ranks, shard_count * up_slab)

    def select_jobs(projected):
        return jnp.sum(projected.reshape(tok_rows, job_slots, ranks) * member[:, :, None], axis=1)

    grad_proj = lax.dot_general(
        grad_output, up_stack, contract_last, preferred_element_type=jnp.float32
    )
    act_proj = lax.dot_general(
        hidden, down_stack, contract_last, preferred_element_type=jnp.float32
    )
    rank_part = jnp.concatenate([select_jobs(grad_proj), select_jobs(act_proj)], axis=1).astype(
        jnp.bfloat16
    )
    weight_pair = lax.all_gather(down_weight, "core", axis=0, tiled=True)
    tokens_same_core = lax.all_gather(grad_output, "chip", axis=0, tiled=True)
    partial_value = lax.dot_general(
        tokens_same_core, weight_pair, contract_last, preferred_element_type=jnp.float32
    )
    routed = lax.all_to_all(
        partial_value.astype(jnp.bfloat16), "chip", split_axis=0, concat_axis=1, tiled=True
    )
    width_here = routed.shape[1] // group_count
    base_grad = lax.psum_scatter(
        routed.reshape(tok_rows, group_count, width_here), "grp", scatter_dimension=1, tiled=True
    ).reshape(tok_rows, width_here)
    rank_sum = lax.psum(rank_part.astype(jnp.float32), "grp")
    grad_rank = rank_sum[:, :ranks].astype(jnp.bfloat16)
    act_rank = rank_sum[:, ranks:].astype(jnp.bfloat16)
    grad_spread = (
        (member[:, :, None] * lax.optimization_barrier(grad_rank).astype(jnp.float32)[:, None, :])
        .reshape(tok_rows, job_slots * ranks)
        .astype(jnp.bfloat16)
    )
    act_spread = (
        (member[:, :, None] * lax.optimization_barrier(act_rank).astype(jnp.float32)[:, None, :])
        .reshape(tok_rows, job_slots * ranks)
        .astype(jnp.bfloat16)
    )
    adapter_term = (
        jnp.dot(grad_spread, down_stack, preferred_element_type=jnp.float32) * ADAPTER_SCALE
    )
    grad_hidden = (base_grad.astype(jnp.float32) + adapter_term).astype(jnp.bfloat16)
    down_rows = lax.dot_general(
        grad_spread, hidden, contract_rows, preferred_element_type=jnp.float32
    )
    down_rows = (down_rows.reshape(job_slots, ranks, -1) * job_weights[:, None, None]).astype(
        jnp.bfloat16
    )
    up_rows = lax.dot_general(
        act_spread, grad_output, contract_rows, preferred_element_type=jnp.float32
    )
    up_rows = (up_rows.reshape(job_slots, ranks, -1) * job_weights[:, None, None]).astype(
        jnp.bfloat16
    )
    returned_down, returned_up = (
        lax.all_to_all(
            down_rows.reshape(job_slots, ranks, shard_count, down_slab),
            SEQ,
            split_axis=2,
            concat_axis=1,
            tiled=True,
        ),
        lax.all_to_all(
            up_rows.reshape(job_slots, ranks, shard_count, up_slab),
            SEQ,
            split_axis=2,
            concat_axis=1,
            tiled=True,
        ),
    )
    tenant_map = (
        tenant_table.transpose(1, 0, 2)
        .reshape(job_slots * shard_count, tenant_total)
        .astype(jnp.bfloat16)
    )
    grad_adapter_down = lax.dot_general(
        tenant_map,
        returned_down.reshape(job_slots * shard_count, ranks * down_slab),
        contract_rows,
        preferred_element_type=jnp.float32,
    ).reshape(tenant_total, ranks, down_slab)
    grad_adapter_up = lax.dot_general(
        tenant_map,
        returned_up.reshape(job_slots * shard_count, ranks * up_slab),
        contract_rows,
        preferred_element_type=jnp.float32,
    ).reshape(tenant_total, ranks, up_slab)
    return (grad_hidden, grad_adapter_down, grad_adapter_up)


SEQ = ("chip", "core")


def solution(mesh):
    chips = mesh.devices.reshape(mesh.shape["grp"], mesh.shape["seq"] // 2, 2)
    mesh = jax.sharding.Mesh(chips, ("grp", "chip", "core"))
    placed = (
        P(SEQ, "grp"),
        P(SEQ, "grp"),
        P(SEQ, "grp"),
        P(None, None, ("grp", "chip", "core")),
        P(None, None, ("grp", "chip", "core")),
        P(),
        P(),
    )
    return jax.shard_map(
        shards,
        mesh=mesh,
        in_specs=placed,
        out_specs=(
            P(SEQ, "grp"),
            P(None, None, ("grp", "chip", "core")),
            P(None, None, ("grp", "chip", "core")),
        ),
        check_vma=False,
    )
```

profile of v0, /device:TPU:32, one launch (start us, length us, event | category | flops | bytes accessed | tf_op | source)
XLA Modules:
  0.0 504.4 jit_solution(12234305566538353482)
XLA Ops:
  7.2 0.0 all-gather.5.cloned.1.call-start
  7.2 0.7 all-gather.5.cloned.1.call-update
  7.9 0.0 all-gather.3.cloned.1.call-start
  8.0 0.7 all-gather.3.cloned.1.call-update
  8.7 0.0 reduce-scatter.2.cloned.1.call-start
  8.7 24.1 %all-gather.5.cloned.1.call-done = bf16[1792,2048]{1,0:T(8,128)(2,1)} async-done(((bf16[896,2048]{1,0:T(8,128)(2,1)}), bf16[1792,2048]{1,0:T(8,128)(2,1)}) %all-gather.5.cloned.1.call-update) | async-done | bytes 7340048 | tf_op jit(solution)/shard_map/all_gather | solution.py:55
  32.8 74.1 %all-gather.3.cloned.1.call-done = bf16[2048,2048]{1,0:T(8,128)(2,1)} async-done(((bf16[128,2048]{1,0:T(8,128)(2,1)}), bf16[2048,2048]{1,0:T(8,128)(2,1)}) %all-gather.3.cloned.1.call-update) | async-done | bytes 8388624 | tf_op jit(solution)/shard_map/all_gather | solution.py:56
  106.9 21.3 %convolution_convert_fusion = bf16[2048,1792]{1,0:T(8,128)(2,1)} fusion(bf16[2048,2048]{1,0:T(8,128)(2,1)} %all-gather.3.cloned.1.call-done, bf16[1792,2048]{1,0:T(8,128)(2,1)} %all-gather.5.cloned.1.call-done), kind=kOutput, calls=%fused_computation.7 | convolution fusion | flops 15036055552 | bytes 23068672 | tf_op jit(solution)/shard_map/dot_general | solution.py:57
  128.2 10.0 %copy.60 = bf16[16,128,1792]{1,2,0:T(8,128)(2,1)} copy(bf16[16,128,1792]{2,1,0:T(8,128)(2,1)} %bitcast.111) | data formatting | bytes 14680064 | tf_op jit(solution)/shard_map/all_to_all | solution.py:60
  138.1 89.2 %all_to_all.76 = bf16[16,128,1792]{1,2,0:T(8,128)(2,1)} all-to-all(bf16[16,128,1792]{1,2,0:T(8,128)(2,1)} %copy.60), channel_id=1, replica_groups=mesh['grp'=4,'chip'=16,'core'=2] {'chip'}, dimensions={0} | all-to-all | bytes 14680064 | tf_op jit(solution)/shard_map/all_to_all | solution.py:60
  227.4 10.0 %copy.61 = bf16[128,4,7168]{2,0,1:T(8,128)(2,1)} copy(bf16[128,4,7168]{0,2,1:T(8,128)(2,1)} %bitcast.104) | data formatting | bytes 14680064 | tf_op jit(solution)/shard_map/reshape | solution.py:65
  237.3 0.0 reduce-scatter.2.cloned.1.call-update
  237.4 0.7 copy-done.6
  238.0 0.1 reshape.139
  238.1 0.5 copy-done.5
  238.6 2.1 gather_fusion
  240.7 3.2 copy.79
  243.9 4.8 reshape.160
  248.7 5.9 %all-to-all-start.1 = ((bf16[32,2,8192]{2,1,0:T(2,128)(2,1)}), bf16[32,2,8192]{2,1,0:T(2,128)(2,1)S(1)}, u32[]{:S(2)}, u32[]{:S(2)}) async-start(bf16[32,2,8192]{2,1,0:T(2,128)(2,1)} %reshape.160), calls=%async_computation.2 | async-start | bytes 2097152 | tf_op jit(solution)/shard_map/all_to_all | solution.py:38
  254.6 2.8 gather_fusion.1
  257.4 4.8 copy.65
  262.2 7.9 %all-to-all-done.1 = bf16[32,2,8192]{2,1,0:T(2,128)(2,1)S(1)} async-done(((bf16[32,2,8192]{2,1,0:T(2,128)(2,1)}), bf16[32,2,8192]{2,1,0:T(2,128)(2,1)S(1)}, u32[]{:S(2)}, u32[]{:S(2)}) %all-to-all-start.1) | async-done | bytes 1048608 | tf_op jit(solution)/shard_map/all_to_all | solution.py:38
  270.1 6.6 %all-to-all-start.2 = ((bf16[4,32,64,224]{3,2,0,1:T(8,128)(2,1)}), bf16[4,32,64,224]{3,2,0,1:T(8,128)(2,1)}, u32[]{:S(2)}, u32[]{:S(2)}) async-start(bf16[4,32,64,224]{3,2,0,1:T(8,128)(2,1)} %copy.65), calls=%async_computation.3 | async-start | bytes 8388608 | tf_op jit(solution)/shard_map/all_to_all | solution.py:37
  276.8 0.1 constant_dynamic-slice_fusion
  276.8 0.1 copy.75
  276.9 0.2 reduce-window.4
  277.1 0.1 iota_compare_fusion
  277.2 0.1 select_reduce_fusion
  277.3 0.1 multiply_reduce_fusion.2
  277.5 0.1 fusion.19
  277.6 1.3 reshape.161
  278.9 0.2 bitcast_bitcast_fusion.1
  279.1 1.4 copy.64
  280.4 2.4 reshape.128
  282.9 1.7 fusion.22
  284.5 46.2 %all-to-all-done.2 = bf16[4,32,64,224]{3,2,0,1:T(8,128)(2,1)} async-done(((bf16[4,32,64,224]{3,2,0,1:T(8,128)(2,1)}), bf16[4,32,64,224]{3,2,0,1:T(8,128)(2,1)}, u32[]{:S(2)}, u32[]{:S(2)}) %all-to-all-start.2) | async-done | bytes 3670048 | tf_op jit(solution)/shard_map/all_to_all | solution.py:37
  330.8 6.6 %copy.66 = bf16[4,1,64,32,224]{4,3,2,0,1:T(8,128)(2,1)} copy(bf16[4,1,64,32,224]{4,2,0,3,1:T(8,128)(2,1)} %bitcast.16) | data formatting | bytes 7340032 | tf_op jit(solution)/shard_map/all_to_all | solution.py:37
  337.4 9.0 %reshape.130 = bf16[256,7168]{1,0:T(8,128)(2,1)} reshape(bf16[4,1,64,32,224]{4,3,2,0,1:T(8,128)(2,1)} %copy.66) | data formatting | bytes 7340032 | tf_op jit(solution)/shard_map/reshape | solution.py:40
  346.3 3.1 fusion.23
  349.5 17.6 %psum.7 = bf16[128,128]{0,1:T(8,128)(2,1)S(1)} all-reduce(f32[128,128]{0,1:T(8,128)S(1)} %maximum_convert_fusion), channel_id=1, replica_groups=mesh['grp'=4,'chip'=16,'core'=2] {'grp'}, use_global_device_ids=true, to_apply=%region_4.5 | all-reduce | flops 16384 | bytes 98304 | tf_op jit(solution)/shard_map/psum | solution.py:67
  367.2 1.4 fusion.3
  368.6 3.3 reshape.134
  372.0 2.1 copy.78
  374.1 4.8 reshape.162
  378.9 5.2 %all-to-all-start.4 = ((bf16[32,2,8192]{2,1,0:T(2,128)(2,1)}), bf16[32,2,8192]{2,1,0:T(2,128)(2,1)S(1)}, u32[]{:S(2)}, u32[]{:S(2)}) async-start(bf16[32,2,8192]{2,1,0:T(2,128)(2,1)} %reshape.162), calls=%async_computation.5 | async-start | bytes 2097152 | tf_op jit(solution)/shard_map/all_to_all | solution.py:104
  384.1 3.0 fusion
  387.1 8.8 %reshape.132 = bf16[4,64,32,224]{3,2,1,0:T(8,128)(2,1)} reshape(bf16[4,64,7168]{2,1,0:T(8,128)(2,1)} %fusion) | data formatting | bytes 7340032 | tf_op jit(solution)/shard_map/reshape | solution.py:98
  395.9 6.6 %copy.67 = bf16[4,64,32,224]{3,1,0,2:T(8,128)(2,1)} copy(bf16[4,64,32,224]{3,2,1,0:T(8,128)(2,1)} %reshape.132) | data formatting | bytes 7340032 | tf_op jit(solution)/shard_map/reshape | solution.py:98
  402.5 7.8 %all-to-all-start.3 = ((bf16[4,64,32,224]{3,1,0,2:T(8,128)(2,1)}), bf16[4,64,32,224]{3,1,0,2:T(8,128)(2,1)}, u32[]{:S(2)}, u32[]{:S(2)}) async-start(bf16[4,64,32,224]{3,1,0,2:T(8,128)(2,1)} %copy.67), calls=%async_computation.4 | async-start | bytes 8388608 | tf_op jit(solution)/shard_map/all_to_all | solution.py:97
  410.4 0.1 eq.23
  410.5 1.3 reshape.163
  411.8 0.2 bitcast_bitcast_fusion
  412.0 0.2 copy.71
  412.2 1.7 reshape.135
  413.9 1.3 copy.72
  415.2 2.3 fusion.12
  417.5 2.5 copy.74
  420.1 44.4 %all-to-all-done.3 = bf16[4,64,32,224]{3,1,0,2:T(8,128)(2,1)} async-done(((bf16[4,64,32,224]{3,1,0,2:T(8,128)(2,1)}), bf16[4,64,32,224]{3,1,0,2:T(8,128)(2,1)}, u32[]{:S(2)}, u32[]{:S(2)}) %all-to-all-start.3) | async-done | bytes 3670048 | tf_op jit(solution)/shard_map/all_to_all | solution.py:97
  464.4 4.8 copy.68
  469.2 8.5 %reshape.133 = bf16[128,14336]{1,0:T(8,128)(2,1)} reshape(bf16[4,32,64,1,224]{4,2,1,0,3:T(8,128)(2,1)} %copy.68) | data formatting | bytes 7340032 | tf_op jit(solution)/shard_map/reshape | solution.py:119
  477.8 6.0 %copy.69 = bf16[14336,128]{1,0:T(8,128)(2,1)} copy(bf16[14336,128]{0,1:T(8,128)(2,1)} %bitcast.107) | data formatting | bytes 7340032 | tf_op jit(solution)/shard_map/dot_general | solution.py:117
  483.8 4.4 fusion.14
  488.2 4.4 copy.73
  492.7 5.0 fusion.2
  (28 shorter events, 0.1 us)
Async XLA Ops:
  7.2 247.4 %copy-start = (bf16[64,64,224]{2,1,0:T(8,128)(2,1)S(1)}, bf16[64,64,224]{2,1,0:T(8,128)(2,1)}, u32[]{:S(2)}) copy-start(bf16[64,64,224]{2,1,0:T(8,128)(2,1)} %param.10) | copy-start | bytes 5505028
  7.2 25.6 %all-gather.5.cloned.1.call-start = ((), (), s32[]{:S(2)}) async-start(), calls=%async_computation.7 | async-start | bytes 11010048 | tf_op jit(solution)/shard_map/all_gather | solution.py:55
  7.9 99.0 %all-gather.3.cloned.1.call-start = ((), (), s32[]{:S(2)}) async-start(), calls=%async_computation.6 | async-start | bytes 8912896 | tf_op jit(solution)/shard_map/all_gather | solution.py:56
  8.7 484.0 %reduce-scatter.2.cloned.1.call-start = ((), (), s32[]{:S(2)}) async-start(), calls=%async_computation.8 | async-start | bytes 9175040 | tf_op jit(solution)/shard_map/reduce_scatter | solution.py:64
  237.3 0.7 copy-start.6
  237.3 1.2 copy-start.5
  248.7 21.5 %all-to-all-start.1 = ((bf16[32,2,8192]{2,1,0:T(2,128)(2,1)}), bf16[32,2,8192]{2,1,0:T(2,128)(2,1)S(1)}, u32[]{:S(2)}, u32[]{:S(2)}) async-start(bf16[32,2,8192]{2,1,0:T(2,128)(2,1)} %reshape.160), calls=%async_computation.2 | async-start | bytes 2097152 | tf_op jit(solution)/shard_map/all_to_all | solution.py:38
  262.2 14.5 %copy-start.7 = (s32[32,4]{0,1:T(4,128)S(1)}, s32[32,4]{0,1:T(4,128)}, u32[]{:S(2)}) copy-start(s32[32,4]{0,1:T(4,128)} %param.13) | copy-start | bytes 1540
  270.1 60.6 %all-to-all-start.2 = ((bf16[4,32,64,224]{3,2,0,1:T(8,128)(2,1)}), bf16[4,32,64,224]{3,2,0,1:T(8,128)(2,1)}, u32[]{:S(2)}, u32[]{:S(2)}) async-start(bf16[4,32,64,224]{3,2,0,1:T(8,128)(2,1)} %copy.65), calls=%async_computation.3 | async-start | bytes 8388608 | tf_op jit(solution)/shard_map/all_to_all | solution.py:37
  279.1 3.8 copy-start.4
  337.4 9.0 %copy-start.2 = (bf16[128,7168]{1,0:T(8,128)(2,1)S(1)}, bf16[128,7168]{1,0:T(8,128)(2,1)}, u32[]{:S(2)}) copy-start(bf16[128,7168]{1,0:T(8,128)(2,1)} %param.8) | copy-start | bytes 5505028
  374.1 10.0 %copy-start.3 = (bf16[128,7168]{1,0:T(8,128)(2,1)S(1)}, bf16[128,7168]{1,0:T(8,128)(2,1)}, u32[]{:S(2)}) copy-start(bf16[128,7168]{1,0:T(8,128)(2,1)} %param.8) | copy-start | bytes 5505028
  378.9 23.7 %all-to-all-start.4 = ((bf16[32,2,8192]{2,1,0:T(2,128)(2,1)}), bf16[32,2,8192]{2,1,0:T(2,128)(2,1)S(1)}, u32[]{:S(2)}, u32[]{:S(2)}) async-start(bf16[32,2,8192]{2,1,0:T(2,128)(2,1)} %reshape.162), calls=%async_computation.5 | async-start | bytes 2097152 | tf_op jit(solution)/shard_map/all_to_all | solution.py:104
  402.5 61.9 %all-to-all-start.3 = ((bf16[4,64,32,224]{3,1,0,2:T(8,128)(2,1)}), bf16[4,64,32,224]{3,1,0,2:T(8,128)(2,1)}, u32[]{:S(2)}, u32[]{:S(2)}) async-start(bf16[4,64,32,224]{3,1,0,2:T(8,128)(2,1)} %copy.67), calls=%async_computation.4 | async-start | bytes 8388608 | tf_op jit(solution)/shard_map/all_to_all | solution.py:97
  492.7 5.0 copy-start.1
Sparse Core Ops, SparseCore 0:
  9.7 23.0 all-gather.4
  34.9 71.9 all-gather.2
  237.5 72.3 reduce-scatter.1
where the time goes:
time: 513 us; the launch traced here: 504 us
  waiting for transfers between devices  198 us (39%)
  local copies, waits for them, and re-layouts  117 us (23%)
  blocking collectives  107 us (21%)
  matrix products  42.2 us (8%)
  starting transfers between devices  25.6 us (5%)
  between operations  14.2 us (3%)
    all_to_all x1, blocking collectives, shards(): lax.all_to_all(partial_value.astype(jnp.bfloat16), 'chip', split_axis=0,...  89.2 us
    all_gather x1, waiting for transfers between devices, shards(): tokens_same_core = lax.all_gather(grad_output, 'chip', axis=0, tiled=True)  74.1 us
    all_to_all x1, waiting for transfers between devices, shards(): lax.all_to_all(adapter_down[chosen], SEQ, split_axis=1, concat_axis=3, ti...  46.2 us
    all_to_all x1, waiting for transfers between devices, shards(): lax.all_to_all(down_rows.reshape(job_slots, ranks, shard_count, down_slab...  44.4 us
    all_gather x1, waiting for transfers between devices, shards(): weight_pair = lax.all_gather(down_weight, 'core', axis=0, tiled=True)  24.1 us
    dot_general x1, matrix products, shards(): lax.dot_general(tokens_same_core, weight_pair, contract_last, preferred_e...  21.3 us
    unnamed x23, local copies, waits for them, and re-layouts  20.5 us
    psum x1, blocking collectives, shards(): rank_sum = lax.psum(rank_part.astype(jnp.float32), 'grp')  17.6 us
  transfers between devices with their start and end apart: 7, of which 5 were waited for; matrix products, arithmetic and copies ran while one was open for 22% of the time, Pallas kernels for 0%

commit v1 on v0

--- a/solution.py
+++ b/solution.py
@@ -52,7 +52,9 @@
     rank_part = jnp.concatenate([select_jobs(grad_proj), select_jobs(act_proj)], axis=1).astype(
         jnp.bfloat16
     )
-    weight_pair = lax.all_gather(down_weight, "core", axis=0, tiled=True)
+    weight_pair = jnp.concatenate(
+        lax.all_to_all(jnp.stack([down_weight] * lax.axis_size("core")), "core", 0, 0), axis=0
+    )
     tokens_same_core = lax.all_gather(grad_output, "chip", axis=0, tiled=True)
     partial_value = lax.dot_general(
         tokens_same_core, weight_pair, contract_last, preferred_element_type=jnp.float32

time: 513 us -> 485 us (0.945)
  waiting for transfers between devices: 198 us -> 159 us
  blocking collectives: 107 us -> 118 us
    all_gather x1 -> x0, waiting for transfers between devices: 24.1 us -> none  [shards(): weight_pair = lax.all_gather(down_weight, 'core', axis=0, tiled=True)]
    all_gather x1, waiting for transfers between devices: 74.1 us -> 60.2 us  [shards(): tokens_same_core = lax.all_gather(grad_output, 'chip', axis=0, tiled=True)]
    all_to_all x0 -> x1, blocking collectives: none -> 10.9 us  [shards(): lax.all_to_all(jnp.stack([down_weight] * lax.axis_size('core')), 'core',...]
  transfers between devices with their start and end apart: 7 -> 6, of which waited for: 5 -> 4; matrix products, arithmetic and copies ran while one was open for 22% -> 24% of each run, Pallas kernels for 0% -> 0%
where the time goes in v1:
time: 485 us; the launch traced here: 476 us
  waiting for transfers between devices  159 us (33%)
  blocking collectives  118 us (24%)
  local copies, waits for them, and re-layouts  112 us (23%)
  matrix products  42.3 us (9%)
  starting transfers between devices  25.6 us (5%)
  between operations  14.5 us (3%)
    all_to_all x1, blocking collectives, shards(): lax.all_to_all(partial_value.astype(jnp.bfloat16), 'chip', split_axis=0,...  89 us
    all_gather x1, waiting for transfers between devices, shards(): tokens_same_core = lax.all_gather(grad_output, 'chip', axis=0, tiled=True)  60.2 us
    all_to_all x1, waiting for transfers between devices, shards(): lax.all_to_all(adapter_down[chosen], SEQ, split_axis=1, concat_axis=3, ti...  46.2 us
    all_to_all x1, waiting for transfers between devices, shards(): lax.all_to_all(down_rows.reshape(job_slots, ranks, shard_count, down_slab...  44.4 us
    dot_general x1, matrix products, shards(): lax.dot_general(tokens_same_core, weight_pair, contract_last, preferred_e...  21.4 us
    unnamed x23, local copies, waits for them, and re-layouts  20.5 us
    psum x1, blocking collectives, shards(): rank_sum = lax.psum(rank_part.astype(jnp.float32), 'grp')  17.6 us
    reshape x2, local copies, waits for them, and re-layouts, shards(): down_rows.reshape(job_slots, ranks, shard_count, down_slab)  15.4 us
  transfers between devices with their start and end apart: 6, of which 4 were waited for; matrix products, arithmetic and copies ran while one was open for 24% of the time, Pallas kernels for 0%

profile of v1, /device:TPU:32, one launch (start us, length us, event | category | flops | bytes accessed | tf_op | source)
XLA Modules:
  0.0 475.7 jit_solution(15583050622166900107)
XLA Ops:
  7.2 0.0 copy-start
  7.2 0.0 all-gather.2.cloned.1.call-start
  7.2 0.7 all-gather.2.cloned.1.call-update
  7.9 0.0 reduce-scatter.2.cloned.1.call-start
  8.0 3.8 pad_maximum_fusion
  11.8 10.9 %all_to_all.81 = bf16[2,896,2048]{2,1,0:T(8,128)(2,1)} all-to-all(bf16[2,896,2048]{2,1,0:T(8,128)(2,1)S(1)} %pad_maximum_fusion), channel_id=1, replica_groups=mesh['grp'=4,'chip'=16,'core'=2] {'core'}, dimensions={0} | all-to-all | bytes 14680064 | tf_op jit(solution)/shard_map/all_to_all | solution.py:56
  22.7 60.2 %all-gather.2.cloned.1.call-done = bf16[2048,2048]{1,0:T(8,128)(2,1)} async-done(((bf16[128,2048]{1,0:T(8,128)(2,1)}), bf16[2048,2048]{1,0:T(8,128)(2,1)}) %all-gather.2.cloned.1.call-update) | async-done | bytes 8388624 | tf_op jit(solution)/shard_map/all_gather | solution.py:58
  82.9 21.4 %fusion.3 = bf16[224,16,8,128]{3,2,1,0:T(8,128)(2,1)} fusion(bf16[1792,2048]{1,0:T(8,128)(2,1)} %bitcast.119, bf16[2048,2048]{1,0:T(8,128)(2,1)} %all-gather.2.cloned.1.call-done), kind=kOutput, calls=%fused_computation.10 | convolution fusion | flops 15036055552 | bytes 23068672 | tf_op jit(solution)/shard_map/dot_general | solution.py:59
  104.3 5.0 %copy.80 = bf16[224,16,8,128]{3,2,0,1:T(8,128)(2,1)S(1)} copy(bf16[224,16,8,128]{3,2,1,0:T(8,128)(2,1)} %fusion.3) | data formatting | bytes 14680064 | tf_op jit(solution)/shard_map/all_to_all | solution.py:62
  109.3 89.0 %all_to_all.82 = bf16[16,128,1792]{1,2,0:T(8,128)(2,1)} all-to-all(bf16[16,128,1792]{1,2,0:T(8,128)(2,1)S(1)} %bitcast.111), channel_id=1, replica_groups=mesh['grp'=4,'chip'=16,'core'=2] {'chip'}, dimensions={0} | all-to-all | bytes 14680064 | tf_op jit(solution)/shard_map/all_to_all | solution.py:62
  198.3 10.0 %copy.61 = bf16[128,4,7168]{2,0,1:T(8,128)(2,1)} copy(bf16[128,4,7168]{0,2,1:T(8,128)(2,1)} %bitcast.112) | data formatting | bytes 14680064 | tf_op jit(solution)/shard_map/reshape | solution.py:67
  208.3 0.0 reduce-scatter.2.cloned.1.call-update
  208.3 0.7 copy-done.6
  209.0 0.1 reshape.143
  209.1 0.5 copy-done.5
  209.6 2.1 gather_fusion
  211.7 3.2 copy.82
  214.8 4.8 %reshape.164 = bf16[32,2,8192]{2,1,0:T(2,128)(2,1)} reshape(bf16[32,4,64,64]{3,2,1,0:T(8,128)(2,1)} %bitcast.116) | data formatting | bytes 2097152
  219.7 5.9 %all-to-all-start.2 = ((bf16[32,2,8192]{2,1,0:T(2,128)(2,1)}), bf16[32,2,8192]{2,1,0:T(2,128)(2,1)S(1)}, u32[]{:S(2)}, u32[]{:S(2)}) async-start(bf16[32,2,8192]{2,1,0:T(2,128)(2,1)} %reshape.164), calls=%async_computation.3 | async-start | bytes 2097152 | tf_op jit(solution)/shard_map/all_to_all | solution.py:38
  225.6 2.8 gather_fusion.1
  228.4 4.8 %copy.65 = bf16[4,32,64,224]{3,2,0,1:T(8,128)(2,1)} copy(bf16[4,32,64,224]{3,2,1,0:T(8,128)(2,1)} %bitcast.113) | data formatting | bytes 7340032 | tf_op jit(solution)/shard_map/gather | solution.py:37
  233.2 7.9 %all-to-all-done.2 = bf16[32,2,8192]{2,1,0:T(2,128)(2,1)S(1)} async-done(((bf16[32,2,8192]{2,1,0:T(2,128)(2,1)}), bf16[32,2,8192]{2,1,0:T(2,128)(2,1)S(1)}, u32[]{:S(2)}, u32[]{:S(2)}) %all-to-all-start.2) | async-done | bytes 1048608 | tf_op jit(solution)/shard_map/all_to_all | solution.py:38
  241.1 6.6 %all-to-all-start.3 = ((bf16[4,32,64,224]{3,2,0,1:T(8,128)(2,1)}), bf16[4,32,64,224]{3,2,0,1:T(8,128)(2,1)}, u32[]{:S(2)}, u32[]{:S(2)}) async-start(bf16[4,32,64,224]{3,2,0,1:T(8,128)(2,1)} %copy.65), calls=%async_computation.4 | async-start | bytes 8388608 | tf_op jit(solution)/shard_map/all_to_all | solution.py:37
  247.7 0.1 constant_dynamic-slice_fusion
  247.8 0.1 copy.75
  247.9 0.2 reduce-window.4
  248.1 0.1 iota_compare_fusion
  248.2 0.1 select_reduce_fusion
  248.3 0.1 multiply_reduce_fusion.2
  248.5 0.1 fusion.20
  248.5 1.3 reshape.165
  249.9 0.2 bitcast_bitcast_fusion.1
  250.1 1.4 copy.64
  251.4 2.4 reshape.132
  253.9 1.7 fusion.23
  255.5 46.2 %all-to-all-done.3 = bf16[4,32,64,224]{3,2,0,1:T(8,128)(2,1)} async-done(((bf16[4,32,64,224]{3,2,0,1:T(8,128)(2,1)}), bf16[4,32,64,224]{3,2,0,1:T(8,128)(2,1)}, u32[]{:S(2)}, u32[]{:S(2)}) %all-to-all-start.3) | async-done | bytes 3670048 | tf_op jit(solution)/shard_map/all_to_all | solution.py:37
  301.8 6.6 %copy.66 = bf16[4,1,64,32,224]{4,3,2,0,1:T(8,128)(2,1)} copy(bf16[4,1,64,32,224]{4,2,0,3,1:T(8,128)(2,1)} %bitcast.18) | data formatting | bytes 7340032 | tf_op jit(solution)/shard_map/all_to_all | solution.py:37
  308.4 8.9 %reshape.134 = bf16[256,7168]{1,0:T(8,128)(2,1)} reshape(bf16[4,1,64,32,224]{4,3,2,0,1:T(8,128)(2,1)} %copy.66) | data formatting | bytes 7340032 | tf_op jit(solution)/shard_map/reshape | solution.py:40
  317.3 3.1 fusion.24
  320.5 17.6 %psum.7 = bf16[128,128]{0,1:T(8,128)(2,1)S(1)} all-reduce(f32[128,128]{0,1:T(8,128)S(1)} %maximum_convert_fusion), channel_id=1, replica_groups=mesh['grp'=4,'chip'=16,'core'=2] {'grp'}, use_global_device_ids=true, to_apply=%region_4.5 | all-reduce | flops 16384 | bytes 98304 | tf_op jit(solution)/shard_map/psum | solution.py:69
  338.2 1.4 fusion.4
  339.6 3.3 reshape.138
  342.9 2.1 copy.81
  345.0 4.8 %reshape.166 = bf16[32,2,8192]{2,1,0:T(2,128)(2,1)} reshape(bf16[32,4,64,64]{3,2,1,0:T(8,128)(2,1)} %bitcast.117) | data formatting | bytes 2097152
  349.8 5.2 %all-to-all-start.5 = ((bf16[32,2,8192]{2,1,0:T(2,128)(2,1)}), bf16[32,2,8192]{2,1,0:T(2,128)(2,1)S(1)}, u32[]{:S(2)}, u32[]{:S(2)}) async-start(bf16[32,2,8192]{2,1,0:T(2,128)(2,1)} %reshape.166), calls=%async_computation.6 | async-start | bytes 2097152 | tf_op jit(solution)/shard_map/all_to_all | solution.py:106
  355.0 3.0 fusion
  358.0 8.8 %reshape.136 = bf16[4,64,32,224]{3,2,1,0:T(8,128)(2,1)} reshape(bf16[4,64,7168]{2,1,0:T(8,128)(2,1)} %fusion) | data formatting | bytes 7340032 | tf_op jit(solution)/shard_map/reshape | solution.py:100
  366.9 6.6 %copy.67 = bf16[4,64,32,224]{3,1,0,2:T(8,128)(2,1)} copy(bf16[4,64,32,224]{3,2,1,0:T(8,128)(2,1)} %reshape.136) | data formatting | bytes 7340032 | tf_op jit(solution)/shard_map/reshape | solution.py:100
  373.5 7.8 %all-to-all-start.4 = ((bf16[4,64,32,224]{3,1,0,2:T(8,128)(2,1)}), bf16[4,64,32,224]{3,1,0,2:T(8,128)(2,1)}, u32[]{:S(2)}, u32[]{:S(2)}) async-start(bf16[4,64,32,224]{3,1,0,2:T(8,128)(2,1)} %copy.67), calls=%async_computation.5 | async-start | bytes 8388608 | tf_op jit(solution)/shard_map/all_to_all | solution.py:99
  381.3 0.1 eq.23
  381.4 1.3 reshape.167
  382.8 0.2 bitcast_bitcast_fusion
  383.0 0.2 copy.71
  383.1 1.7 reshape.139
  384.8 1.3 copy.72
  386.1 2.3 fusion.13
  388.5 2.5 copy.74
  391.0 44.4 %all-to-all-done.4 = bf16[4,64,32,224]{3,1,0,2:T(8,128)(2,1)} async-done(((bf16[4,64,32,224]{3,1,0,2:T(8,128)(2,1)}), bf16[4,64,32,224]{3,1,0,2:T(8,128)(2,1)}, u32[]{:S(2)}, u32[]{:S(2)}) %all-to-all-start.4) | async-done | bytes 3670048 | tf_op jit(solution)/shard_map/all_to_all | solution.py:99
  435.4 4.8 %copy.68 = bf16[4,32,64,1,224]{4,2,1,0,3:T(8,128)(2,1)} copy(bf16[4,32,64,1,224]{4,2,0,1,3:T(8,128)(2,1)} %bitcast.28) | data formatting | bytes 7340032 | tf_op jit(solution)/shard_map/all_to_all | solution.py:99
  440.2 8.5 %reshape.137 = bf16[128,14336]{1,0:T(8,128)(2,1)} reshape(bf16[4,32,64,1,224]{4,2,1,0,3:T(8,128)(2,1)} %copy.68) | data formatting | bytes 7340032 | tf_op jit(solution)/shard_map/reshape | solution.py:121
  448.7 6.0 %copy.69 = bf16[14336,128]{1,0:T(8,128)(2,1)} copy(bf16[14336,128]{0,1:T(8,128)(2,1)} %bitcast.115) | data formatting | bytes 7340032 | tf_op jit(solution)/shard_map/dot_general | solution.py:119
  454.7 4.4 fusion.15
  459.1 4.5 copy.73
  463.6 5.0 %fusion.2 = bf16[128,7168]{1,0:T(8,128)(2,1)} fusion(bf16[128,256]{0,1:T(8,128)(2,1)S(1)} %bitcast.125, bf16[256,7168]{1,0:T(8,128)(2,1)} %reshape.134, bf16[128,1,7168]{2,0,1:T(8,128)(2,1)} %reduce-scatter.2.cloned.1.call-done), kind=kOutput, calls=%fused_computation.6 | convolution fusion | flops 473432064 | bytes 7405568 | tf_op jit(solution)/shard_map/dot_general | solution.py:83
  (27 shorter events, 0.1 us)
Async XLA Ops:
  7.2 218.4 %copy-start = (bf16[64,64,224]{2,1,0:T(8,128)(2,1)S(1)}, bf16[64,64,224]{2,1,0:T(8,128)(2,1)}, u32[]{:S(2)}) copy-start(bf16[64,64,224]{2,1,0:T(8,128)(2,1)} %param.10) | copy-start | bytes 5505028
  7.2 75.7 %all-gather.2.cloned.1.call-start = ((), (), s32[]{:S(2)}) async-start(), calls=%async_computation.7 | async-start | bytes 8912896 | tf_op jit(solution)/shard_map/all_gather | solution.py:58
  7.9 455.7 %reduce-scatter.2.cloned.1.call-start = ((), (), s32[]{:S(2)}) async-start(), calls=%async_computation.8 | async-start | bytes 9175040 | tf_op jit(solution)/shard_map/reduce_scatter | solution.py:66
  208.3 0.7 copy-start.6
  208.3 1.2 copy-start.5
  219.7 21.5 %all-to-all-start.2 = ((bf16[32,2,8192]{2,1,0:T(2,128)(2,1)}), bf16[32,2,8192]{2,1,0:T(2,128)(2,1)S(1)}, u32[]{:S(2)}, u32[]{:S(2)}) async-start(bf16[32,2,8192]{2,1,0:T(2,128)(2,1)} %reshape.164), calls=%async_computation.3 | async-start | bytes 2097152 | tf_op jit(solution)/shard_map/all_to_all | solution.py:38
  233.2 14.5 %copy-start.7 = (s32[32,4]{0,1:T(4,128)S(1)}, s32[32,4]{0,1:T(4,128)}, u32[]{:S(2)}) copy-start(s32[32,4]{0,1:T(4,128)} %param.13) | copy-start | bytes 1540
  241.1 60.6 %all-to-all-start.3 = ((bf16[4,32,64,224]{3,2,0,1:T(8,128)(2,1)}), bf16[4,32,64,224]{3,2,0,1:T(8,128)(2,1)}, u32[]{:S(2)}, u32[]{:S(2)}) async-start(bf16[4,32,64,224]{3,2,0,1:T(8,128)(2,1)} %copy.65), calls=%async_computation.4 | async-start | bytes 8388608 | tf_op jit(solution)/shard_map/all_to_all | solution.py:37
  250.1 3.8 copy-start.4
  308.4 8.9 %copy-start.2 = (bf16[128,7168]{1,0:T(8,128)(2,1)S(1)}, bf16[128,7168]{1,0:T(8,128)(2,1)}, u32[]{:S(2)}) copy-start(bf16[128,7168]{1,0:T(8,128)(2,1)} %param.8) | copy-start | bytes 5505028
  345.0 10.0 %copy-start.3 = (bf16[128,7168]{1,0:T(8,128)(2,1)S(1)}, bf16[128,7168]{1,0:T(8,128)(2,1)}, u32[]{:S(2)}) copy-start(bf16[128,7168]{1,0:T(8,128)(2,1)} %param.8) | copy-start | bytes 5505028
  349.8 23.7 %all-to-all-start.5 = ((bf16[32,2,8192]{2,1,0:T(2,128)(2,1)}), bf16[32,2,8192]{2,1,0:T(2,128)(2,1)S(1)}, u32[]{:S(2)}, u32[]{:S(2)}) async-start(bf16[32,2,8192]{2,1,0:T(2,128)(2,1)} %reshape.166), calls=%async_computation.6 | async-start | bytes 2097152 | tf_op jit(solution)/shard_map/all_to_all | solution.py:106
  373.5 61.9 %all-to-all-start.4 = ((bf16[4,64,32,224]{3,1,0,2:T(8,128)(2,1)}), bf16[4,64,32,224]{3,1,0,2:T(8,128)(2,1)}, u32[]{:S(2)}, u32[]{:S(2)}) async-start(bf16[4,64,32,224]{3,1,0,2:T(8,128)(2,1)} %copy.67), calls=%async_computation.5 | async-start | bytes 8388608 | tf_op jit(solution)/shard_map/all_to_all | solution.py:99
  463.6 5.0 %copy-start.1 = (bf16[64,64,224]{2,1,0:T(8,128)(2,1)S(1)}, bf16[64,64,224]{2,1,0:T(8,128)(2,1)}, u32[]{:S(2)}) copy-start(bf16[64,64,224]{2,1,0:T(8,128)(2,1)} %param.10) | copy-start | bytes 5505028
Sparse Core Ops, SparseCore 0:
  10.2 72.6 all-gather.1
  208.5 72.2 reduce-scatter.1
